TPU v7x, 256 devices: a whole 4x4x8 slice. The times are simulated.
256 devices in a mesh: dp: 8 (over x_lo, y), owner: 8 (over z), context: 4 (over x_hi, core).
Axes of the slice: x: 4 (x_hi: 2, x_lo: 2; x = x_hi * 2 + x_lo), y: 4, z: 8, core: 2. Of those that a mesh axis runs over, the one named last changes fastest.
Arguments:
- grad_partials: bfloat16 [32, 1536, 64, 192], P(('dp', 'context'), None, 'owner')
- assignment: int32 [64, 1], replicated, may hold values from 0 to 7; in each aligned block of 8 rows (0 to 7, 8 to 15, ...) at most 2 rows name the same one
- momentum: float32 [128, 1536, 192], P('owner', ('dp', 'context')), may hold values from -6 to 6
- q_weight: float32 [128, 1536, 192], P('owner', ('dp', 'context')), may hold values from -1.2 to 1.2
- k_weight: float32 [64, 512, 128], P('owner', ('dp', 'context')), may hold values from -6 to 6
- max_logits: float32 [4, 64], P('context'), may hold values from 20 to 400
Outputs:
- momentum_out: float32 [128, 1536, 192], P('owner', ('dp', 'context'))
- q_weight_out: float32 [128, 1536, 192], P('owner', ('dp', 'context'))
- k_weight_out: float32 [64, 512, 128], P('owner', ('dp', 'context'))
Inputs may be any that keep to these rules, and one draw needn't show every extreme that they name: `assignment`: in each aligned block of 8 heads no owner index is named more than 2 times, and some owner index exactly 2 times.
All inputs are finite; a program needn't handle non-finite values.
Results may differ from a plain program's by a relative error of at most 0.0007.
Values may be sent and summed in bfloat16 or wider, within the bound.
A program may use at most 128 MiB of HBM per device.

v0:
```python
import math
import jax
import jax.numpy as jnp
from jax import lax
from jax.sharding import PartitionSpec as P

QR = 1536
QK = 192
ITERS = 2
MOMENTUM_RATE = 0.95
WEIGHT_KEEP = 0.98
LOGIT_CAP = 100.0
QUINTIC_A = 3.4445
QUINTIC_B = -4.775
QUINTIC_C = 2.0315


def routing(assignment, heads_own, per_source):
    target = assignment[:, 0]
    head_index = jnp.arange(target.shape[0], dtype=jnp.int32)
    source_block = head_index // heads_own
    earlier = (
        (source_block[None, :] == source_block[:, None])
        & (head_index[None, :] < head_index[:, None])
        & (target[None, :] == target[:, None])
    )
    position = jnp.sum(earlier.astype(jnp.int32), axis=1)
    return (target, position, source_block * per_source + position)


def refresh(weight, orthogonal, gamma, kn_count):
    step_size = 0.04 * math.sqrt(max(QR, QK))
    column_index = jnp.arange(weight.shape[2])
    column_scale = jnp.where(
        column_index[None, :] < kn_count, jnp.sqrt(gamma)[:, None], gamma[:, None]
    )
    return (WEIGHT_KEEP * weight - step_size * orthogonal.astype(jnp.float32)) * column_scale[
        :, None, :
    ]


def quintic(whole):
    for step in range(ITERS):
        gram_matrix = jnp.einsum("nrk,nrl->nkl", whole, whole, preferred_element_type=jnp.float32)
        polynomial = (
            QUINTIC_B * gram_matrix
            + QUINTIC_C
            * jnp.einsum("nkl,nlm->nkm", gram_matrix, gram_matrix, precision=lax.Precision.HIGHEST)
        ).astype(jnp.bfloat16)
        whole = (
            QUINTIC_A * whole.astype(jnp.float32)
            + jnp.einsum("nrk,nkl->nrl", whole, polynomial, preferred_element_type=jnp.float32)
        ).astype(jnp.bfloat16)
    return whole


def orthogonalize(matrix):
    square_sum = lax.psum(jnp.sum(matrix * matrix, axis=(1, 2)), ("dp", "context"))
    iterate = (matrix / (jnp.sqrt(square_sum) + 1e-07)[:, None, None]).astype(jnp.bfloat16)
    row_count = matrix.shape[1]
    gathered = lax.all_gather(iterate, ("dp", "context"), axis=1, tiled=True)
    gathered = quintic(gathered)
    return lax.dynamic_slice_in_dim(
        gathered, lax.axis_index(("dp", "context")) * row_count, row_count, 1
    )


def body(grad_partials, assignment, momentum, q_weight, k_weight, max_logits):
    heads_own = grad_partials.shape[2]
    slots_own = momentum.shape[0]
    kn_count = k_weight.shape[2]
    per_source = slots_own // lax.axis_size("owner")
    my_owner = lax.axis_index("owner")
    target, position, local_slot = routing(assignment, heads_own, per_source)
    peak_logit = lax.pmax(max_logits[0], "context")
    gamma = jnp.minimum(1.0, LOGIT_CAP / peak_logit)
    partial_value = grad_partials[0]
    grad_rows = lax.psum_scatter(
        partial_value.astype(jnp.float32), ("dp", "context"), scatter_dimension=0, tiled=True
    )
    home_target = lax.dynamic_slice_in_dim(target, my_owner * heads_own, heads_own)
    home_position = lax.dynamic_slice_in_dim(position, my_owner * heads_own, heads_own)
    send_index = home_target * per_source + home_position
    slot_index = jnp.arange(slots_own, dtype=jnp.int32)
    sender = (slot_index[:, None] == send_index[None, :]).astype(jnp.float32)
    owned_mask = (
        (target[None, :] == my_owner) & (local_slot[None, :] == slot_index[:, None])
    ).astype(jnp.float32)
    occupied = (jnp.sum(owned_mask, axis=1) > 0.5)[:, None, None]
    home_gamma = lax.dynamic_slice_in_dim(gamma, my_owner * heads_own, heads_own)
    outgoing = jnp.einsum("qi,rik->qrk", sender, grad_rows, precision=lax.Precision.HIGHEST)
    arrived = lax.all_to_all(outgoing, "owner", split_axis=0, concat_axis=0, tiled=True)
    refreshed = jnp.where(occupied, MOMENTUM_RATE * momentum + arrived, momentum)
    orthogonal = orthogonalize(refreshed)
    slot_gamma = jnp.sum(owned_mask * gamma[None, :], axis=1)
    slot_gamma = jnp.where(occupied[:, 0, 0], slot_gamma, 1.0)
    q_weight_out = jnp.where(
        occupied, refresh(q_weight, orthogonal, slot_gamma, kn_count), q_weight
    )
    k_weight_out = k_weight * jnp.sqrt(home_gamma)[:, None, None]
    return (refreshed, q_weight_out, k_weight_out)


def solution(mesh):
    placed = (
        P(("dp", "context"), None, "owner", None),
        P(),
        P("owner", ("dp", "context"), None),
        P("owner", ("dp", "context"), None),
        P("owner", ("dp", "context"), None),
        P("context", None),
    )
    return jax.shard_map(
        body,
        mesh=mesh,
        in_specs=placed,
        out_specs=(
            P("owner", ("dp", "context"), None),
            P("owner", ("dp", "context"), None),
            P("owner", ("dp", "context"), None),
        ),
        check_vma=False,
    )
```

profile of v0, /device:TPU:1, one launch (start us, length us, event | category | flops | bytes accessed | tf_op | source)
XLA Modules:
  0.0 456.4 jit_solution(1013946448971146130)
XLA Ops:
  7.2 0.0 reduce-scatter.2.cloned.1.call-start
  7.2 9.2 %copy.57 = bf16[1,1536,8,192]{3,2,1,0:T(8,128)(2,1)} copy(bf16[1,1536,8,192]{1,3,2,0:T(8,128)(2,1)} %param.6) | data formatting | bytes 9437184 | tf_op args[0]
  16.4 7.5 %bitcast_convert_fusion = f32[1536,8,192]{2,1,0:T(8,128)} fusion(bf16[1,1536,8,192]{3,2,1,0:T(8,128)(2,1)} %copy.57), kind=kLoop, calls=%fused_computation.4 | loop fusion | flops 2359296 | bytes 14155776 | tf_op jit(solution)/shard_map/convert_element_type | solution.py:79
  23.8 0.0 copy-start.4
  23.8 0.0 reduce-scatter.2.cloned.1.call-update
  23.9 0.0 copy-start.5
  23.9 0.0 copy-start.1
  23.9 0.6 copy-done.4
  24.5 0.2 convert_reduce_fusion
  24.7 0.1 fusion.13
  24.7 175.2 %reduce-scatter.2.cloned.1.call-done = f32[48,8,192]{2,1,0:T(8,128)} async-done(((f32[1536,8,192]{2,1,0:T(8,128)}), f32[48,8,192]{2,1,0:T(8,128)}) %reduce-scatter.2.cloned.1.call-update) | async-done | bytes 294928 | tf_op jit(solution)/shard_map/reduce_scatter | solution.py:78
  199.9 1.6 fusion.8
  201.5 1.3 copy.58
  202.9 0.0 copy-start.3
  202.9 8.6 %all-to-all-start = ((f32[16,48,192]{2,1,0:T(8,128)}), f32[16,48,192]{2,1,0:T(8,128)S(1)}, u32[]{:S(2)}, u32[]{:S(2)}) async-start(f32[16,48,192]{2,1,0:T(8,128)} %copy.58), calls=%async_computation.1 | async-start | bytes 1572864 | tf_op jit(solution)/shard_map/all_to_all | solution.py:92
  211.5 0.0 all-gather.2.cloned.1.call-start
  211.5 0.0 copy-done.5
  211.5 10.9 %pmax.7 = f32[64]{0:T(128)S(1)} all-reduce(f32[64]{0:T(128)S(1)} %bitcast.24), channel_id=1, replica_groups=mesh['dp'=8,'owner'=8,'context'=4] {'context'}, use_global_device_ids=true, to_apply=%region_5.6 | all-reduce | flops 64 | bytes 512 | tf_op jit(solution)/shard_map/pmax | solution.py:75
  222.4 0.1 select_reduce_fusion
  222.5 8.9 %all-to-all-done = f32[16,48,192]{2,1,0:T(8,128)S(1)} async-done(((f32[16,48,192]{2,1,0:T(8,128)}), f32[16,48,192]{2,1,0:T(8,128)S(1)}, u32[]{:S(2)}, u32[]{:S(2)}) %all-to-all-start) | async-done | bytes 589856 | tf_op jit(solution)/shard_map/all_to_all | solution.py:92
  231.4 0.0 copy-done.1
  231.4 0.3 multiply_reduce_fusion
  231.7 0.0 copy-start
  231.8 66.2 %psum.7 = f32[16]{0:T(128)S(1)} all-reduce(f32[16]{0:T(128)S(1)} %get-tuple-element.16), channel_id=1, replica_groups=mesh['dp'=8,'owner'=8,'context'=4] {'dp','context'}, use_global_device_ids=true, to_apply=%region_4.5 | all-reduce | flops 16 | bytes 128 | tf_op jit(solution)/shard_map/psum | solution.py:58
  297.9 0.1 divide_convert_fusion
  298.1 0.9 copy.59
  298.9 0.0 all-gather.2.cloned.1.call-update
  299.0 0.1 dynamic-slice_sqrt_fusion
  299.1 0.1 broadcast_select_fusion
  299.1 0.0 copy-done.3
  299.1 0.7 broadcast_multiply_fusion
  299.9 73.1 %all-gather.2.cloned.1.call-done = bf16[16,1536,192]{2,0,1:T(8,128)(2,1)} async-done(((bf16[16,48,192]{2,0,1:T(8,128)(2,1)}), bf16[16,1536,192]{2,0,1:T(8,128)(2,1)}) %all-gather.2.cloned.1.call-update) | async-done | bytes 9437200 | tf_op jit(solution)/shard_map/all_gather | solution.py:61
  373.0 21.7 %fusion = f32[16,192,192]{2,1,0:T(8,128)S(1)} fusion(bf16[16,1536,192]{2,0,1:T(8,128)(2,1)} %all-gather.2.cloned.1.call-done), kind=kOutput, calls=%fused_computation.1 | convolution fusion | flops 1811939328 | bytes 11796480 | tf_op jit(solution)/shard_map/nrk,nrl->nkl/dot_general | solution.py:44
  394.7 0.0 copy-done
  394.7 3.6 add_convert_fusion.2
  398.3 17.7 %add_convert_fusion = bf16[16,1536,192]{2,1,0:T(8,128)(2,1)} fusion(bf16[16,192,192]{2,1,0:T(8,128)(2,1)S(1)} %add_convert_fusion.2, bf16[16,1536,192]{2,0,1:T(8,128)(2,1)} %all-gather.2.cloned.1.call-done), kind=kOutput, calls=%fused_computation | convolution fusion | flops 1830813696 | bytes 20054016 | tf_op jit(solution)/shard_map/nrk,nkl->nrl/dot_general | solution.py:52
  416.0 11.3 %fusion.15 = f32[16,192,192]{2,1,0:T(8,128)S(1)} fusion(bf16[16,1536,192]{2,1,0:T(8,128)(2,1)} %add_convert_fusion), kind=kOutput, calls=%fused_computation.44 | convolution fusion | flops 1811939328 | bytes 11796480 | tf_op jit(solution)/shard_map/nrk,nrl->nkl/dot_general | solution.py:44
  427.4 3.5 add_convert_fusion.1
  430.8 0.0 copy-start.2
  430.9 16.4 %fusion.16 = f32[16,1536,192]{2,1,0:T(8,128)} fusion(bf16[16,1536,192]{2,1,0:T(8,128)(2,1)} %add_convert_fusion, bf16[16,192,192]{2,1,0:T(8,128)(2,1)S(1)} %add_convert_fusion.1), kind=kOutput, calls=%fused_computation.45 | convolution fusion | flops 1811939328 | bytes 29491200 | tf_op jit(solution)/shard_map/nrk,nkl->nrl/dot_general | solution.py:52
  447.2 0.0 copy-done.2
  447.2 2.4 multiply_select_fusion
  (8 shorter events, 0.0 us)
Async XLA Ops:
  7.2 192.8 %reduce-scatter.2.cloned.1.call-start = ((), (), s32[]{:S(2)}) async-start(), calls=%async_computation.2 | async-start | bytes 12976128 | tf_op jit(solution)/shard_map/reduce_scatter | solution.py:78
  23.8 0.7 copy-start.4
  23.9 187.7 %copy-start.5 = (f32[1,64]{1,0:T(1,128)S(1)}, f32[1,64]{1,0:T(1,128)}, u32[]{:S(2)}) copy-start(f32[1,64]{1,0:T(1,128)} %param.11) | copy-start | bytes 772
  23.9 207.6 %copy-start.1 = (f32[16,48,192]{2,1,0:T(8,128)S(1)}, f32[16,48,192]{2,1,0:T(8,128)}, u32[]{:S(2)}) copy-start(f32[16,48,192]{2,1,0:T(8,128)} %param.8) | copy-start | bytes 1769476
  202.9 96.3 %copy-start.3 = (f32[8,16,128]{2,1,0:T(8,128)S(1)}, f32[8,16,128]{2,1,0:T(8,128)}, u32[]{:S(2)}) copy-start(f32[8,16,128]{2,1,0:T(8,128)} %param.10) | copy-start | bytes 196612
  202.9 28.6 %all-to-all-start = ((f32[16,48,192]{2,1,0:T(8,128)}), f32[16,48,192]{2,1,0:T(8,128)S(1)}, u32[]{:S(2)}, u32[]{:S(2)}) async-start(f32[16,48,192]{2,1,0:T(8,128)} %copy.58), calls=%async_computation.1 | async-start | bytes 1572864 | tf_op jit(solution)/shard_map/all_to_all | solution.py:92
  211.5 161.5 %all-gather.2.cloned.1.call-start = ((), (), s32[]{:S(2)}) async-start(), calls=%async_computation.3 | async-start | bytes 12976128 | tf_op jit(solution)/shard_map/all_gather | solution.py:61
  231.7 163.0 %copy-start = (f32[16,48,192]{2,1,0:T(8,128)}, f32[16,48,192]{2,1,0:T(8,128)S(1)}, u32[]{:S(2)}) copy-start(f32[16,48,192]{2,1,0:T(8,128)S(1)} %get-tuple-element.17) | copy-start | bytes 1769476
  430.8 16.4 %copy-start.2 = (f32[16,48,192]{2,1,0:T(8,128)S(1)}, f32[16,48,192]{2,1,0:T(8,128)}, u32[]{:S(2)}) copy-start(f32[16,48,192]{2,1,0:T(8,128)} %param.9) | copy-start | bytes 1769476
Sparse Core Ops, SparseCore 0:
  24.0 175.8 reduce-scatter.1
  299.1 73.8 all-gather.1
where the time goes:
time: 457 us; the launch traced here: 456 us
  waiting for transfers between devices  257 us (56%)
  blocking collectives  77 us (17%)
  matrix products  75.8 us (17%)
  between operations  14.2 us (3%)
  local copies, waits for them, and re-layouts  12.1 us (3%)
  other arithmetic  11.5 us (3%)
  starting transfers between devices  8.69 us (2%)
    reduce_scatter x1, waiting for transfers between devices, body(): lax.psum_scatter(partial_value.astype(jnp.float32), ('dp', 'context'), sc...  175 us
    all_gather x1, waiting for transfers between devices, orthogonalize(): gathered = lax.all_gather(iterate, ('dp', 'context'), axis=1, tiled=True)  73.1 us
    psum x1, blocking collectives, orthogonalize(): lax.psum(jnp.sum(matrix * matrix, axis=(1, 2)), ('dp', 'context'))  66.2 us
    dot_general x2, matrix products, quintic(): jnp.einsum('nrk,nkl->nrl', whole, polynomial, preferred_element_type=jnp....  34.1 us
    dot_general x2, matrix products, quintic(): jnp.einsum('nrk,nrl->nkl', whole, whole, preferred_element_type=jnp.float32)  33.1 us
    pmax x1, blocking collectives, body(): peak_logit = lax.pmax(max_logits[0], 'context')  10.9 us
    unnamed x13, local copies, waits for them, and re-layouts  9.79 us
  transfers between devices with their start and end apart: 3, of which 3 were waited for; matrix products, arithmetic and copies ran while one was open for 0% of the time, Pallas kernels for 0%

commit v1 on v0

--- a/solution.py
+++ b/solution.py
@@ -55,7 +55,7 @@
 
 
 def orthogonalize(matrix):
-    square_sum = lax.psum(jnp.sum(matrix * matrix, axis=(1, 2)), ("dp", "context"))
+    square_sum = lax.psum(lax.psum(jnp.sum(matrix * matrix, axis=(1, 2)), "context"), "dp")
     iterate = (matrix / (jnp.sqrt(square_sum) + 1e-07)[:, None, None]).astype(jnp.bfloat16)
     row_count = matrix.shape[1]
     gathered = lax.all_gather(iterate, ("dp", "context"), axis=1, tiled=True)

time: 457 us -> 419 us (0.917)
  blocking collectives: 77 us -> 35.1 us
    psum x1 -> x2, blocking collectives: 66.2 us -> 24.2 us  [the longest x1 13.5 us: orthogonalize(): lax.psum(lax.psum(jnp.sum(matrix * matrix, axis=(1, 2)), 'context'), 'dp')]
where the time goes in v1:
time: 419 us; the launch traced here: 418 us
  waiting for transfers between devices  261 us (62%)
  matrix products  75.8 us (18%)
  blocking collectives  35.1 us (8%)
  between operations  14.2 us (3%)
  local copies, waits for them, and re-layouts  12.1 us (3%)
  other arithmetic  11.5 us (3%)
  starting transfers between devices  8.69 us (2%)
    reduce_scatter x1, waiting for transfers between devices, body(): lax.psum_scatter(partial_value.astype(jnp.float32), ('dp', 'context'), sc...  175 us
    all_gather x1, waiting for transfers between devices, orthogonalize(): gathered = lax.all_gather(iterate, ('dp', 'context'), axis=1, tiled=True)  76.8 us
    dot_general x2, matrix products, quintic(): jnp.einsum('nrk,nkl->nrl', whole, polynomial, preferred_element_type=jnp....  34.1 us
    dot_general x2, matrix products, quintic(): jnp.einsum('nrk,nrl->nkl', whole, whole, preferred_element_type=jnp.float32)  33.1 us
    psum x1, blocking collectives, orthogonalize(): lax.psum(lax.psum(jnp.sum(matrix * matrix, axis=(1, 2)), 'context'), 'dp')  13.5 us
    pmax x1, blocking collectives, body(): peak_logit = lax.pmax(max_logits[0], 'context')  10.9 us
    psum x1, blocking collectives, orthogonalize(): lax.psum(jnp.sum(matrix * matrix, axis=(1, 2)), 'context')  10.7 us
    unnamed x13, local copies, waits for them, and re-layouts  9.79 us
  transfers between devices with their start and end apart: 3, of which 3 were waited for; matrix products, arithmetic and copies ran while one was open for 0% of the time, Pallas kernels for 0%

profile of v1, /device:TPU:1, one launch (start us, length us, event | category | flops | bytes accessed | tf_op | source)
XLA Modules:
  0.0 418.2 jit_solution(2990450678348707835)
XLA Ops:
  7.2 0.0 reduce-scatter.2.cloned.1.call-start
  7.2 9.2 %copy.57 = bf16[1,1536,8,192]{3,2,1,0:T(8,128)(2,1)} copy(bf16[1,1536,8,192]{1,3,2,0:T(8,128)(2,1)} %param.6) | data formatting | bytes 9437184 | tf_op args[0]
  16.4 7.5 %bitcast_convert_fusion = f32[1536,8,192]{2,1,0:T(8,128)} fusion(bf16[1,1536,8,192]{3,2,1,0:T(8,128)(2,1)} %copy.57), kind=kLoop, calls=%fused_computation.4 | loop fusion | flops 2359296 | bytes 14155776 | tf_op jit(solution)/shard_map/convert_element_type | solution.py:79
  23.8 0.0 copy-start.4
  23.8 0.0 reduce-scatter.2.cloned.1.call-update
  23.9 0.0 copy-start.5
  23.9 0.0 copy-start.1
  23.9 0.6 copy-done.4
  24.5 0.2 convert_reduce_fusion
  24.7 0.1 fusion.13
  24.7 175.2 %reduce-scatter.2.cloned.1.call-done = f32[48,8,192]{2,1,0:T(8,128)} async-done(((f32[1536,8,192]{2,1,0:T(8,128)}), f32[48,8,192]{2,1,0:T(8,128)}) %reduce-scatter.2.cloned.1.call-update) | async-done | bytes 294928 | tf_op jit(solution)/shard_map/reduce_scatter | solution.py:78
  199.9 1.6 fusion.8
  201.5 1.3 copy.58
  202.9 0.0 copy-start.3
  202.9 8.6 %all-to-all-start = ((f32[16,48,192]{2,1,0:T(8,128)}), f32[16,48,192]{2,1,0:T(8,128)S(1)}, u32[]{:S(2)}, u32[]{:S(2)}) async-start(f32[16,48,192]{2,1,0:T(8,128)} %copy.58), calls=%async_computation.1 | async-start | bytes 1572864 | tf_op jit(solution)/shard_map/all_to_all | solution.py:92
  211.5 0.0 all-gather.2.cloned.1.call-start
  211.5 0.0 copy-done.5
  211.5 10.9 %pmax.7 = f32[64]{0:T(128)S(1)} all-reduce(f32[64]{0:T(128)S(1)} %bitcast.24), channel_id=1, replica_groups=mesh['dp'=8,'owner'=8,'context'=4] {'context'}, use_global_device_ids=true, to_apply=%region_6.7 | all-reduce | flops 64 | bytes 512 | tf_op jit(solution)/shard_map/pmax | solution.py:75
  222.4 0.1 select_reduce_fusion
  222.5 8.9 %all-to-all-done = f32[16,48,192]{2,1,0:T(8,128)S(1)} async-done(((f32[16,48,192]{2,1,0:T(8,128)}), f32[16,48,192]{2,1,0:T(8,128)S(1)}, u32[]{:S(2)}, u32[]{:S(2)}) %all-to-all-start) | async-done | bytes 589856 | tf_op jit(solution)/shard_map/all_to_all | solution.py:92
  231.4 0.0 copy-done.1
  231.4 0.3 multiply_reduce_fusion
  231.7 0.0 copy-start
  231.8 10.7 %psum.14 = f32[16]{0:T(128)S(1)} all-reduce(f32[16]{0:T(128)S(1)} %get-tuple-element.16), channel_id=1, replica_groups=mesh['dp'=8,'owner'=8,'context'=4] {'context'}, use_global_device_ids=true, to_apply=%region_4.5 | all-reduce | flops 16 | bytes 128 | tf_op jit(solution)/shard_map/psum | solution.py:58
  242.4 13.5 %psum.15 = f32[16]{0:T(128)S(1)} all-reduce(f32[16]{0:T(128)S(1)} %psum.14), channel_id=1, replica_groups=mesh['dp'=8,'owner'=8,'context'=4] {'dp'}, use_global_device_ids=true, to_apply=%region_5.6 | all-reduce | flops 16 | bytes 128 | tf_op jit(solution)/shard_map/psum | solution.py:58
  256.0 0.1 divide_convert_fusion
  256.1 0.9 copy.59
  257.0 0.0 all-gather.2.cloned.1.call-update
  257.0 0.1 dynamic-slice_sqrt_fusion
  257.1 0.1 broadcast_select_fusion
  257.2 0.0 copy-done.3
  257.2 0.7 broadcast_multiply_fusion
  257.9 76.8 %all-gather.2.cloned.1.call-done = bf16[16,1536,192]{2,0,1:T(8,128)(2,1)} async-done(((bf16[16,48,192]{2,0,1:T(8,128)(2,1)}), bf16[16,1536,192]{2,0,1:T(8,128)(2,1)}) %all-gather.2.cloned.1.call-update) | async-done | bytes 9437200 | tf_op jit(solution)/shard_map/all_gather | solution.py:61
  334.7 21.7 %fusion = f32[16,192,192]{2,1,0:T(8,128)S(1)} fusion(bf16[16,1536,192]{2,0,1:T(8,128)(2,1)} %all-gather.2.cloned.1.call-done), kind=kOutput, calls=%fused_computation.1 | convolution fusion | flops 1811939328 | bytes 11796480 | tf_op jit(solution)/shard_map/nrk,nrl->nkl/dot_general | solution.py:44
  356.4 0.0 copy-done
  356.4 3.6 add_convert_fusion.2
  360.1 17.7 %add_convert_fusion = bf16[16,1536,192]{2,1,0:T(8,128)(2,1)} fusion(bf16[16,192,192]{2,1,0:T(8,128)(2,1)S(1)} %add_convert_fusion.2, bf16[16,1536,192]{2,0,1:T(8,128)(2,1)} %all-gather.2.cloned.1.call-done), kind=kOutput, calls=%fused_computation | convolution fusion | flops 1830813696 | bytes 20054016 | tf_op jit(solution)/shard_map/nrk,nkl->nrl/dot_general | solution.py:52
  377.8 11.3 %fusion.15 = f32[16,192,192]{2,1,0:T(8,128)S(1)} fusion(bf16[16,1536,192]{2,1,0:T(8,128)(2,1)} %add_convert_fusion), kind=kOutput, calls=%fused_computation.44 | convolution fusion | flops 1811939328 | bytes 11796480 | tf_op jit(solution)/shard_map/nrk,nrl->nkl/dot_general | solution.py:44
  389.1 3.5 add_convert_fusion.1
  392.6 0.0 copy-start.2
  392.6 16.4 %fusion.16 = f32[16,1536,192]{2,1,0:T(8,128)} fusion(bf16[16,1536,192]{2,1,0:T(8,128)(2,1)} %add_convert_fusion, bf16[16,192,192]{2,1,0:T(8,128)(2,1)S(1)} %add_convert_fusion.1), kind=kOutput, calls=%fused_computation.45 | convolution fusion | flops 1811939328 | bytes 29491200 | tf_op jit(solution)/shard_map/nrk,nkl->nrl/dot_general | solution.py:52
  408.9 0.0 copy-done.2
  409.0 2.4 multiply_select_fusion
  (8 shorter events, 0.0 us)
Async XLA Ops:
  7.2 192.8 %reduce-scatter.2.cloned.1.call-start = ((), (), s32[]{:S(2)}) async-start(), calls=%async_computation.2 | async-start | bytes 12976128 | tf_op jit(solution)/shard_map/reduce_scatter | solution.py:78
  23.8 0.7 copy-start.4
  23.9 187.7 %copy-start.5 = (f32[1,64]{1,0:T(1,128)S(1)}, f32[1,64]{1,0:T(1,128)}, u32[]{:S(2)}) copy-start(f32[1,64]{1,0:T(1,128)} %param.11) | copy-start | bytes 772
  23.9 207.6 %copy-start.1 = (f32[16,48,192]{2,1,0:T(8,128)S(1)}, f32[16,48,192]{2,1,0:T(8,128)}, u32[]{:S(2)}) copy-start(f32[16,48,192]{2,1,0:T(8,128)} %param.8) | copy-start | bytes 1769476
  202.9 54.3 %copy-start.3 = (f32[8,16,128]{2,1,0:T(8,128)S(1)}, f32[8,16,128]{2,1,0:T(8,128)}, u32[]{:S(2)}) copy-start(f32[8,16,128]{2,1,0:T(8,128)} %param.10) | copy-start | bytes 196612
  202.9 28.6 %all-to-all-start = ((f32[16,48,192]{2,1,0:T(8,128)}), f32[16,48,192]{2,1,0:T(8,128)S(1)}, u32[]{:S(2)}, u32[]{:S(2)}) async-start(f32[16,48,192]{2,1,0:T(8,128)} %copy.58), calls=%async_computation.1 | async-start | bytes 1572864 | tf_op jit(solution)/shard_map/all_to_all | solution.py:92
  211.5 123.2 %all-gather.2.cloned.1.call-start = ((), (), s32[]{:S(2)}) async-start(), calls=%async_computation.3 | async-start | bytes 12976128 | tf_op jit(solution)/shard_map/all_gather | solution.py:61
  231.7 124.7 %copy-start = (f32[16,48,192]{2,1,0:T(8,128)}, f32[16,48,192]{2,1,0:T(8,128)S(1)}, u32[]{:S(2)}) copy-start(f32[16,48,192]{2,1,0:T(8,128)S(1)} %get-tuple-element.17) | copy-start | bytes 1769476
  392.6 16.4 %copy-start.2 = (f32[16,48,192]{2,1,0:T(8,128)S(1)}, f32[16,48,192]{2,1,0:T(8,128)}, u32[]{:S(2)}) copy-start(f32[16,48,192]{2,1,0:T(8,128)} %param.9) | copy-start | bytes 1769476
Sparse Core Ops, SparseCore 0:
  24.0 175.8 reduce-scatter.1
  257.1 77.5 all-gather.1
